TPU v7x, 512 devices: a whole 4x4x16 slice. The times are simulated.
512 devices in a mesh: tm: 32 (over z_lo, x), wall: 16 (over z_hi, y, core).
Axes of the slice: x: 4, y: 4, z: 16 (z_hi: 2, z_lo: 8; z = z_hi * 8 + z_lo), core: 2. Of those that a mesh axis runs over, the one named last changes fastest.
Arguments:
- start_state: float32 [32, 3, 384, 2048], P('tm', None, 'wall'), may hold values from -6 to 6
- end_state: float32 [32, 3, 384, 2048], P('tm', None, None, 'wall'), may hold values from -6 to 6
- coupling: float32 [32, 3, 384, 2048], P('tm', None, None, 'wall'), may hold values from 0.5 to 1.5
- inverse_ops: float32 [32, 384, 384], P('wall')
- mirror_rows: int32 [384], replicated, may hold values from 0 to 383, as said below
- slab_steps: int32 [32], P('tm'), may hold values from 1 to 8, as said below
Outputs:
- gradient: float32 [32, 3, 384, 2048], P('tm', None, 'wall')
Inputs may be any that keep to these rules, and one draw needn't show every extreme that they name: mirror_rows is an involution that maps each row of block b = y // 24 to a row of block 15 - b. `slab_steps`: some slab takes 8 steps.
All inputs are finite; a program needn't handle non-finite values.
Results may differ from a plain program's by a relative error of at most 0.00028.
Values sent between devices are 32-bit elements; how exact they have to be, the bound alone decides.
A program may use at most 64 MiB of HBM per device.

v0:
```python
import jax
import jax.numpy as jnp
from jax import lax
from jax.sharding import PartitionSpec as P

STEPS_MAX = 8


def shifted(value, axis, steps):
    count = lax.axis_size(axis)
    pairs = [(source, (source + steps) % count) for source in range(count)]
    return lax.ppermute(value, axis, pairs)


def mirror(values, mirror_rows):
    parity = jnp.array([1.0, -1.0, 1.0], jnp.float32).reshape(1, 3, 1, 1)
    return jnp.take(values, mirror_rows, axis=2) * parity


def helmholtz(values, inverse_ops):
    slab_count, components, row_count, col_count = values.shape
    groups = inverse_ops.shape[0]
    blocked = values.reshape(slab_count, components, row_count, groups, col_count // groups)
    product = jnp.einsum("gyz,sczgm->scygm", inverse_ops, blocked, precision=lax.Precision.HIGHEST)
    return product.reshape(values.shape)


def adjoint(mismatch, coupling, inverse_ops, slab_steps):
    step_count = slab_steps[0]
    adjoint_state = mismatch
    for position in range(STEPS_MAX):
        advanced = helmholtz(coupling * adjoint_state, inverse_ops)
        adjoint_state = jnp.where(position < step_count, advanced, adjoint_state)
    return adjoint_state


def on_device(start_state, end_state, coupling, inverse_ops, mirror_rows, slab_steps):
    following = shifted(start_state, "tm", -1)
    following_modes = lax.all_to_all(following, "wall", split_axis=3, concat_axis=2, tiled=True)
    mismatch = end_state - mirror(following_modes, mirror_rows)
    adjoint_state = adjoint(mismatch, coupling, inverse_ops, slab_steps)
    earlier = shifted(mirror(mismatch, mirror_rows), "tm", 1)
    gradient_modes = adjoint_state - earlier
    gradient = lax.all_to_all(gradient_modes, "wall", split_axis=2, concat_axis=3, tiled=True)
    return gradient


def solution(mesh):
    in_specs = (
        P("tm", None, "wall", None),
        P("tm", None, None, "wall"),
        P("tm", None, None, "wall"),
        P("wall", None, None),
        P(),
        P("tm"),
    )
    out_specs = P("tm", None, "wall", None)
    return jax.shard_map(
        on_device, mesh=mesh, in_specs=in_specs, out_specs=out_specs, check_vma=False
    )
```

profile of v0, /device:TPU:1, one launch (start us, length us, event | category | flops | bytes accessed | tf_op | source)
XLA Modules:
  0.0 175.5 jit_solution(17240055337523774500)
XLA Ops:
  0.0 16.0 %collective-permute-start = (f32[1,3,24,2048]{3,2,1,0:T(8,128)}, f32[1,3,24,2048]{3,2,1,0:T(8,128)S(1)}, u32[]{:S(2)}, u32[]{:S(2)}) collective-permute-start(f32[1,3,24,2048]{3,2,1,0:T(8,128)} %param.10), channel_id=1, source_target_pairs={{0,496},{16,0},{32,16},{48,32},{64,48},{80,64},{96,80},{112,96},{1... | collective-permute-start | bytes 1769480 | tf_op jit(solution)/shard_map/ppermute | solution.py:12
  16.0 12.3 %collective-permute-done = f32[1,3,24,2048]{3,2,1,0:T(8,128)S(1)} collective-permute-done((f32[1,3,24,2048]{3,2,1,0:T(8,128)}, f32[1,3,24,2048]{3,2,1,0:T(8,128)S(1)}, u32[]{:S(2)}, u32[]{:S(2)}) %collective-permute-start) | collective-permute-done | bytes 589856 | tf_op jit(solution)/shard_map/ppermute | solution.py:12
  28.3 3.1 %copy.305 = f32[1,3,24,2048]{2,1,0,3:T(4,128)} copy(f32[1,3,24,2048]{3,2,1,0:T(8,128)S(1)} %collective-permute-done) | data formatting | bytes 1179648 | tf_op jit(solution)/shard_map/ppermute | solution.py:12
  31.4 5.7 %reshape.156 = f32[16,1,9216]{2,1,0:T(1,128)} reshape(f32[2048,1,3,24]{3,2,1,0:T(4,128)} %bitcast.104) | data formatting | bytes 1179648
  37.1 11.9 %all-to-all-start = ((f32[16,1,9216]{2,1,0:T(1,128)}), f32[16,1,9216]{2,1,0:T(1,128)S(1)}, u32[]{:S(2)}, u32[]{:S(2)}) async-start(f32[16,1,9216]{2,1,0:T(1,128)} %reshape.156), calls=%async_computation | async-start | bytes 1179648 | tf_op jit(solution)/shard_map/all_to_all | solution.py:39
  49.7 26.4 %all-to-all-done = f32[16,1,9216]{2,1,0:T(1,128)S(1)} async-done(((f32[16,1,9216]{2,1,0:T(1,128)}), f32[16,1,9216]{2,1,0:T(1,128)S(1)}, u32[]{:S(2)}, u32[]{:S(2)}) %all-to-all-start) | async-done | bytes 589856 | tf_op jit(solution)/shard_map/all_to_all | solution.py:39
  76.1 0.5 broadcast.29
  76.6 2.0 %reduce = f32[16,9216]{1,0:T(8,128)S(1)} reduce(f32[16,1,9216]{2,1,0:T(1,128)S(1)} %all-to-all-done, f32[]{:T(128)} %broadcast.29), dimensions={1}, to_apply=%all_to_all.26.reduce_sub_computation | reduce | bytes 1179652 | tf_op jit(solution)/shard_map/all_to_all | solution.py:39
  78.7 4.3 %reshape.157 = f32[2048,1,3,24]{3,2,1,0:T(4,128)} reshape(f32[16,9216]{1,0:T(8,128)S(1)} %reduce) | data formatting | bytes 1179648
  83.0 4.4 %copy.306 = f32[1,3,24,2048]{3,0,2,1:T(1,128)S(1)} copy(f32[1,3,24,2048]{2,1,0,3:T(4,128)} %bitcast.105) | data formatting | bytes 1179648 | tf_op jit(solution)/shard_map/all_to_all | solution.py:39
  87.7 1.3 copy.369
  89.0 2.4 %gather_fusion = f32[384,3,128]{2,1,0:T(4,128)S(1)} fusion(f32[3,384,128]{2,0,1:T(4,128)} %bitcast.107, s32[1024]{0:T(1024)S(1)} %pad_clamp_fusion), kind=kCustom, calls=%fused_computation.clone | custom fusion | bytes 1181184 | tf_op jit(solution)/shard_map/jit(_take)/gather | solution.py:17
  91.4 2.1 %fusion.26 = (f32[1,3,384,128]{3,2,1,0:T(8,128)}, f32[1,3,384,128]{3,2,1,0:T(8,128)S(1)}) fusion(f32[1,3,384,128]{3,2,1,0:T(8,128)S(1)} %copy-done.1, f32[1,3,384,128]{3,2,1,0:T(8,128)} %param.11, f32[3]{0:T(128)S(1)} %copy-done.5, f32[384,3,128]{2,1,0:T(4,128)S(1)} %gather_fusion, pred[384]{0:T(512)(128)(4,1)S(1)} %compare_and_fusion), kind=kLoop, calls=%fused_computation.50 | loop fusion | flops 589824 | bytes 2949516 | tf_op jit(solution)/shard_map/mul | solution.py:32
  93.5 1.3 copy.342
  94.8 2.4 %gather_fusion.1 = f32[384,3,128]{2,1,0:T(4,128)S(1)} fusion(f32[3,384,128]{2,0,1:T(4,128)} %copy.342, s32[1024]{0:T(1024)S(1)} %pad_clamp_fusion), kind=kCustom, calls=%fused_computation.1.clone | custom fusion | bytes 1181184 | tf_op jit(solution)/shard_map/jit(_take)/gather | solution.py:17
  97.2 0.9 fusion.8
  98.1 2.1 %collective-permute-start.1 = (f32[1,3,384,128]{3,2,1,0:T(8,128)}, f32[1,3,384,128]{3,2,1,0:T(8,128)}, u32[]{:S(2)}, u32[]{:S(2)}) collective-permute-start(f32[1,3,384,128]{3,2,1,0:T(8,128)} %fusion.8), channel_id=1, source_target_pairs={{0,16},{16,32},{32,48},{48,64},{64,80},{80,96},{96,112},{112,128},... | collective-permute-start | bytes 1769480 | tf_op jit(solution)/shard_map/ppermute | solution.py:12
  100.2 1.3 copy.310
  101.5 1.5 convolution_bitcast_fusion.7
  103.1 0.2 copy.313
  103.4 1.1 copy.314
  104.5 2.6 %convolution_bitcast_fusion.6 = f32[1,3,384,2,64]{2,4,1,3,0:T(8,128)S(1)} fusion(f32[2,384,384]{2,1,0:T(8,128)S(1)} %copy-done, f32[3,384,2,64]{1,3,2,0:T(8,128)} %bitcast.121), kind=kOutput, calls=%fused_computation.8 | convolution fusion | flops 679477248 | bytes 2359296 | tf_op jit(solution)/shard_map/gyz,sczgm->scygm/dot_general | solution.py:24
  107.1 1.1 copy.317
  108.2 2.0 %fusion.25 = (f32[1,3,384,128]{3,2,1,0:T(8,128)}, f32[1,3,384,128]{3,2,1,0:T(8,128)S(1)}) fusion(f32[1,3,384,128]{3,2,1,0:T(8,128)S(1)} %copy-done.1, f32[1,3,384,128]{3,2,1,0:T(8,128)} %copy.317, f32[1,3,384,128]{3,2,1,0:T(8,128)S(1)} %copy.313, f32[1,3,384,128]{3,2,1,0:T(8,128)S(1)} %get-tuple-element.13, pred[]{:T(512)} %bitcast.7, pred[]{:T(512)} %bitcast.6), kind=kLoop, calls=%fused_computation.49 | loop fusion | flops 442368 | bytes 3538946 | tf_op jit(solution)/shard_map/mul | solution.py:32
  110.2 1.3 copy.318
  111.5 1.5 convolution_bitcast_fusion.5
  113.1 0.2 copy.321
  113.4 1.1 copy.322
  114.4 2.6 %convolution_bitcast_fusion.4 = f32[1,3,384,2,64]{2,4,1,3,0:T(8,128)S(1)} fusion(f32[2,384,384]{2,1,0:T(8,128)S(1)} %copy-done, f32[3,384,2,64]{1,3,2,0:T(8,128)} %bitcast.123), kind=kOutput, calls=%fused_computation.6 | convolution fusion | flops 679477248 | bytes 2359296 | tf_op jit(solution)/shard_map/gyz,sczgm->scygm/dot_general | solution.py:24
  117.1 1.1 copy.325
  118.1 0.9 fusion.24
  119.1 1.5 copy.326
  120.6 1.5 convolution_bitcast_fusion.3
  122.2 0.2 copy.329
  122.5 0.2 copy.330
  122.7 1.5 convolution_bitcast_fusion.2
  124.3 1.3 copy.333
  125.6 0.9 fusion.23
  126.5 1.3 copy.334
  127.8 1.5 convolution_bitcast_fusion.1
  129.4 0.2 copy.337
  129.8 0.2 copy.338
  130.0 1.5 convolution_bitcast_fusion
  131.6 0.2 copy.341
  131.8 1.2 select_subtract_fusion
  133.0 0.6 copy.344
  133.6 40.7 %all_to_all.36 = f32[1,3,384,128]{3,0,1,2:T(1,128)S(1)} all-to-all(f32[1,3,384,128]{3,0,1,2:T(1,128)S(1)} %copy.344), channel_id=1, replica_groups=mesh['tm'=32,'wall'=16] {'wall'}, dimensions={2} | all-to-all | bytes 1179648 | tf_op jit(solution)/shard_map/all_to_all | solution.py:44
  174.5 1.0 copy.347
  (31 shorter events, 1.0 us)
Async XLA Ops:
  0.0 101.5 %copy-start = (f32[2,384,384]{2,1,0:T(8,128)S(1)}, f32[2,384,384]{2,1,0:T(8,128)}, u32[]{:S(2)}) copy-start(f32[2,384,384]{2,1,0:T(8,128)} %param.13) | copy-start | bytes 3538948
  0.0 28.3 %collective-permute-start = (f32[1,3,24,2048]{3,2,1,0:T(8,128)}, f32[1,3,24,2048]{3,2,1,0:T(8,128)S(1)}, u32[]{:S(2)}, u32[]{:S(2)}) collective-permute-start(f32[1,3,24,2048]{3,2,1,0:T(8,128)} %param.10), channel_id=1, source_target_pairs={{0,496},{16,0},{32,16},{48,32},{64,48},{80,64},{96,80},{112,96},{1... | collective-permute-start | bytes 1769480 | tf_op jit(solution)/shard_map/ppermute | solution.py:12
  37.1 12.6 %copy-start.4 = (s32[384]{0:T(512)S(1)}, s32[384]{0:T(512)}, u32[]{:S(2)}) copy-start(s32[384]{0:T(512)} %param.14) | copy-start | bytes 4612
  37.1 39.1 %all-to-all-start = ((f32[16,1,9216]{2,1,0:T(1,128)}), f32[16,1,9216]{2,1,0:T(1,128)S(1)}, u32[]{:S(2)}, u32[]{:S(2)}) async-start(f32[16,1,9216]{2,1,0:T(1,128)} %reshape.156), calls=%async_computation | async-start | bytes 1179648 | tf_op jit(solution)/shard_map/all_to_all | solution.py:39
  87.7 3.7 %copy-start.1 = (f32[1,3,384,128]{3,2,1,0:T(8,128)S(1)}, f32[1,3,384,128]{3,2,1,0:T(8,128)}, u32[]{:S(2)}) copy-start(f32[1,3,384,128]{3,2,1,0:T(8,128)} %param.12) | copy-start | bytes 1769476
  87.7 3.7 %copy-start.5 = (f32[3]{0:T(128)S(1)}, f32[3]{0:T(128)}, u32[]{:S(2)}) copy-start(f32[3]{0:T(128)} %constant.36.clone) | copy-start | bytes 40
  98.1 33.7 %collective-permute-start.1 = (f32[1,3,384,128]{3,2,1,0:T(8,128)}, f32[1,3,384,128]{3,2,1,0:T(8,128)}, u32[]{:S(2)}, u32[]{:S(2)}) collective-permute-start(f32[1,3,384,128]{3,2,1,0:T(8,128)} %fusion.8), channel_id=1, source_target_pairs={{0,16},{16,32},{32,48},{48,64},{64,80},{80,96},{96,112},{112,128},... | collective-permute-start | bytes 1769480 | tf_op jit(solution)/shard_map/ppermute | solution.py:12
  119.1 3.3 %copy-start.2 = (f32[1,3,384,128]{3,2,1,0:T(8,128)}, f32[1,3,384,128]{3,2,1,0:T(8,128)S(1)}, u32[]{:S(2)}) copy-start(f32[1,3,384,128]{3,2,1,0:T(8,128)S(1)} %get-tuple-element.9) | copy-start | bytes 1769476
  124.3 1.3 copy-start.3
where the time goes:
time: 179 us; the launch traced here: 175 us
  blocking collectives  40.7 us (23%)
  local copies, waits for them, and re-layouts  40.1 us (22%)
  waiting for transfers between devices  38.7 us (22%)
  starting transfers between devices  30 us (17%)
  matrix products  14.4 us (8%)
  other arithmetic  10.4 us (6%)
    all_to_all x1, blocking collectives, on_device(): lax.all_to_all(gradient_modes, 'wall', split_axis=2, concat_axis=3, tiled...  40.7 us
    all_to_all x1, waiting for transfers between devices, on_device(): lax.all_to_all(following, 'wall', split_axis=3, concat_axis=2, tiled=True)  26.4 us
    ppermute x2, starting transfers between devices, shifted(): return lax.ppermute(value, axis, pairs)  18.1 us
    dot_general x8, matrix products, helmholtz(): jnp.einsum('gyz,sczgm->scygm', inverse_ops, blocked, precision=lax.Precis...  14.4 us
    ppermute x2, waiting for transfers between devices, shifted(): return lax.ppermute(value, axis, pairs)  12.3 us
    all_to_all x1, starting transfers between devices, on_device(): lax.all_to_all(following, 'wall', split_axis=3, concat_axis=2, tiled=True)  11.9 us
    unnamed x14, local copies, waits for them, and re-layouts  10 us
    mul x8, local copies, waits for them, and re-layouts, adjoint(): advanced = helmholtz(coupling * adjoint_state, inverse_ops)  7.94 us
  transfers between devices with their start and end apart: 3, of which 2 were waited for; matrix products, arithmetic and copies ran while one was open for 18% of the time, Pallas kernels for 0%

commit v1 on v0

v1 whole, which is shorter than its diff:
```python
import functools

import jax
import jax.numpy as jnp
from jax import lax
from jax.experimental import pallas as pl
from jax.experimental.pallas import tpu as pltpu
from jax.sharding import PartitionSpec as P

STEPS = 8
NY = 384
ROWS = 24
LANES = 128
WALL = 16
CHUNKS = ((0, 2), (2, 1))
SIGN = (1.0, -1.0, 1.0)
DETOUR = ((0, 0), (0, 1), (1, 0))
MESH = pl.DeviceIdType.MESH
F32 = jnp.float32
BF16 = jnp.bfloat16


def place():
    tm = lax.axis_index("tm")
    wall = lax.axis_index("wall")
    x = lax.rem(tm, 4)
    y = lax.rem(lax.div(wall, 2), 4)
    core = lax.rem(wall, 2)
    z = lax.div(wall, 8) * 8 + lax.div(tm, 4)
    return x, y, z, core


def device_at(x, y, z, core):
    x, y, z, core = lax.rem(x, 4), lax.rem(y, 4), lax.rem(z, 16), lax.rem(core, 2)
    return lax.rem(z, 8) * 4 + x, lax.div(z, 8) * 8 + y * 2 + core


def halves(value):
    high = value.astype(BF16)
    return high, (value - high.astype(F32)).astype(BF16)


def permuted(onehot, value):
    high = value.astype(BF16)
    rest = value - high.astype(F32)
    middle, low = halves(rest)
    dot = functools.partial(jnp.dot, preferred_element_type=F32)
    return (dot(onehot, high) + dot(onehot, middle)) + dot(onehot, low)


def kernel(start_ref, end_ref, coupling_ref, ops_ref, mirror_ref, steps_ref, out_ref,
           land, end_land, end_send, end_v, coup_v, ops_v, wcat, xcat, onehot, state, result,
           local_sem, send_sem, land_sem, end_sem, out_sem, own_sem):
    x, y, z, core = place()
    wall = lax.axis_index("wall")
    first = x == 0
    last = x == 3
    behind = jnp.where(first, 1, 0)
    z_next = lax.div(z, 8) * 8 + lax.rem(z + 1, 8)
    z_prev = lax.div(z, 8) * 8 + lax.rem(z + 7, 8)

    loads = [
        pltpu.make_async_copy(end_ref, end_v, local_sem.at[0]),
        pltpu.make_async_copy(ops_ref, ops_v, local_sem.at[1]),
        pltpu.make_async_copy(coupling_ref, coup_v, local_sem.at[2]),
    ]
    for load in loads:
        load.start()

    barrier = pltpu.get_barrier_semaphore()

    def greet(device):
        pl.semaphore_signal(barrier, inc=1, device_id=device, device_id_type=MESH)

    pairs = [(dy, dc) for dy in range(4) for dc in range(2)]
    ahead = jnp.where(last, 1, 0)
    for half in (8, 0):
        for dy, dc in pairs:
            greet(device_at(x + 3, y + dy, z + half + 16 - behind, core + dc))
            greet(device_at(x + 1, y + dy, z + half + ahead, core + dc))
            if half or dy or dc:
                greet(device_at(x, y + dy, z + half, core + dc))

    @pl.when(first)
    def _():
        for dy, dc in DETOUR:
            greet(device_at(x, y + dy, z + 14, core + dc))
            greet(device_at(x, y + 4 - dy, z + 2, core + dc))
        greet(device_at(x + 3, y, z + 9, core))
        greet(device_at(x + 1, y, z_prev, core))
        greet(device_at(x + 2, y, z_prev, core))

    @pl.when(last)
    def _():
        greet(device_at(x + 1, y, z + 7, core))
        greet(device_at(x + 2, y, z, core))
        greet(device_at(x + 3, y, z, core))

    @pl.when(x == 1)
    def _():
        greet(device_at(x + 2, y, z, core))
        greet(device_at(x + 3, y, z_next, core))

    @pl.when(x == 2)
    def _():
        greet(device_at(x + 1, y, z, core))
        greet(device_at(x + 2, y, z_next, core))

    extra = jnp.where(first, 2 * len(DETOUR) + 3, jnp.where(last, 3, 2))
    pl.semaphore_wait(barrier, 47 + extra)

    sends = []
    for index, (comp, count) in enumerate(CHUNKS):
        for half in (8, 0):
            order = pairs if not half else list(DETOUR) + [p for p in pairs if p not in DETOUR]
            for dy, dc in order:
                tm_to, wall_to = device_at(x + 3, y + dy, z + half + 16 - behind, core + dc)
                column = pl.multiple_of(wall_to * LANES, LANES)
                row, sem = wall * ROWS, index * (WALL + 3) + wall
                if half and (dy, dc) in DETOUR:
                    number = DETOUR.index((dy, dc))
                    tm_by, wall_by = device_at(x, y + dy, z + 14, core + dc)
                    tm_to = jnp.where(first, tm_by, tm_to)
                    wall_to = jnp.where(first, wall_by, wall_to)
                    row = jnp.where(first, NY + number * ROWS, row)
                    sem = jnp.where(first, index * (WALL + 3) + WALL + number, sem)
                send = pltpu.make_async_remote_copy(
                    start_ref.at[pl.ds(comp, count), :, pl.ds(column, LANES)],
                    land.at[pl.ds(comp, count), pl.ds(pl.multiple_of(row, 8), ROWS), :],
                    send_sem.at[0], land_sem.at[sem], device_id=(tm_to, wall_to), device_id_type=MESH)
                send.start()
                sends.append(send)

    lane = lax.broadcasted_iota(jnp.int32, (NY, LANES), 1)
    lower = lane < 64
    source = lax.broadcasted_iota(jnp.int32, (NY, NY), 0)
    onehot[...] = jnp.where(source == mirror_ref[...], 1.0, 0.0).astype(BF16)
    loads[0].wait()
    for comp in range(3):
        end_send[comp] = permuted(onehot[...], end_v[comp]) * SIGN[comp]
    for comp in range(3):
        slot, sem = comp, comp
        tm_to, wall_to = device_at(x + 1, y, jnp.where(last, z_next, z), core)
        if comp:
            tm_by, wall_by = device_at(x + 1 + comp, y, z, core)
            tm_to = jnp.where(last, tm_by, tm_to)
            wall_to = jnp.where(last, wall_by, wall_to)
            slot = jnp.where(last, 3, comp)
        send = pltpu.make_async_remote_copy(
            end_send.at[comp], end_land.at[slot], send_sem.at[1], end_sem.at[slot],
            device_id=(tm_to, wall_to), device_id_type=MESH)
        send.start()
        sends.append(send)
    loads[1].wait()
    for group in range(2):
        high, low = halves(ops_v[group])
        rows = slice(group * NY, (group + 1) * NY)
        wcat[rows, 0:NY] = high
        wcat[rows, NY:2 * NY] = low
        wcat[rows, 2 * NY:3 * NY] = high
    loads[2].wait()

    def arrival(ref, sem):
        return pltpu.make_async_remote_copy(
            ref, ref, send_sem.at[2], sem, device_id=(lax.axis_index("tm"), wall), device_id_type=MESH)

    def passing(index):
        comp, count = CHUNKS[index]
        copies = []
        for number, (dy, dc) in enumerate(DETOUR):
            _, wall_from = device_at(x, y + 4 - dy, z + 2, core + dc)
            held = land.at[pl.ds(comp, count), pl.ds(NY + number * ROWS, ROWS), :]
            copies.append((held, index * (WALL + 3) + WALL + number, pltpu.make_async_remote_copy(
                held, land.at[pl.ds(comp, count), pl.ds(pl.multiple_of(wall_from * ROWS, 8), ROWS), :],
                send_sem.at[2], land_sem.at[index * (WALL + 3) + wall_from],
                device_id=device_at(x + 3, y, z + 9, core), device_id_type=MESH)))
        return copies

    @pl.when(first)
    def _():
        for index in range(len(CHUNKS)):
            for held, sem, copy in passing(index):
                arrival(held, land_sem.at[sem]).wait_recv()
                copy.start()

    @pl.when((x == 1) | (x == 2))
    def _():
        arrival(end_land.at[3], end_sem.at[3]).wait_recv()
        pltpu.make_async_remote_copy(
            end_land.at[3], end_land.at[x], send_sem.at[2], end_sem.at[x],
            device_id=device_at(4 + x * 0, y, z_next, core), device_id_type=MESH).start()

    def leaving(index, half, dy, dc):
        comp, count = CHUNKS[index]
        tm_to, wall_to = device_at(x, y + dy, z + half, core + dc)
        return pltpu.make_async_remote_copy(
            result.at[pl.ds(comp, count), pl.ds(pl.multiple_of(wall_to * ROWS, 8), ROWS), :],
            out_ref.at[pl.ds(comp, count), :, pl.ds(pl.multiple_of(wall * LANES, LANES), LANES)],
            send_sem.at[3], out_sem.at[index * WALL + wall], device_id=(tm_to, wall_to), device_id_type=MESH)

    def staying(index):
        comp, count = CHUNKS[index]
        return pltpu.make_async_copy(
            result.at[pl.ds(comp, count), pl.ds(pl.multiple_of(wall * ROWS, 8), ROWS), :],
            out_ref.at[pl.ds(comp, count), :, pl.ds(pl.multiple_of(wall * LANES, LANES), LANES)],
            own_sem.at[index])

    steps = steps_ref[0]
    for index, (comp, count) in enumerate(CHUNKS):
        for place_from in range(WALL):
            arrival(land.at[pl.ds(comp, count), pl.ds(place_from * ROWS, ROWS), :],
                    land_sem.at[index * (WALL + 3) + place_from]).wait_recv()
        comps = range(comp, comp + count)
        width = count * LANES
        for at, c in enumerate(comps):
            state[:, at * LANES:(at + 1) * LANES] = end_v[c] - permuted(onehot[...], land[c, 0:NY, :]) * SIGN[c]

        def step(number, carry, comps=comps, width=width):
            for at, c in enumerate(comps):
                lanes = slice(at * LANES, (at + 1) * LANES)
                high, low = halves(coup_v[c] * state[:, lanes])
                xcat[0:NY, lanes] = high
                xcat[NY:2 * NY, lanes] = high
                xcat[2 * NY:3 * NY, lanes] = low
            both = jnp.dot(wcat[...], xcat[:, 0:width], preferred_element_type=F32)
            for at, c in enumerate(comps):
                lanes = slice(at * LANES, (at + 1) * LANES)
                advanced = jnp.where(lower, both[0:NY, lanes], both[NY:2 * NY, lanes])
                state[:, lanes] = jnp.where(number < steps, advanced, state[:, lanes])
            return carry

        lax.fori_loop(0, STEPS, step, 0)
        for at, c in enumerate(comps):
            arrival(end_land.at[c], end_sem.at[c]).wait_recv()
            result[c] = state[:, at * LANES:(at + 1) * LANES] - end_land[c]
        for half in (8, 0):
            for dy, dc in pairs:
                if half or dy or dc:
                    leaving(index, half, dy, dc).start()
        staying(index).start()

    for index, (comp, count) in enumerate(CHUNKS):
        staying(index).wait()
        for half in (8, 0):
            for dy, dc in pairs:
                if half or dy or dc:
                    _, wall_from = device_at(x, y + dy, z + half, core + dc)
                    arrival(out_ref.at[pl.ds(comp, count), :, pl.ds(pl.multiple_of(wall_from * LANES, LANES), LANES)],
                            out_sem.at[index * WALL + wall_from]).wait_recv()
                    leaving(index, half, dy, dc).wait_send()
    for send in sends:
        send.wait_send()

    @pl.when(first)
    def _():
        for index in range(len(CHUNKS)):
            for _, _, copy in passing(index):
                copy.wait_send()

    @pl.when((x == 1) | (x == 2))
    def _():
        arrival(end_land.at[3], end_sem.at[3]).wait_send()


def on_device(start_state, end_state, coupling, inverse_ops, mirror_rows, slab_steps):
    anywhere = pl.BlockSpec(memory_space=pl.ANY)
    start = start_state[0]
    arrived = pl.pallas_call(
        kernel,
        out_shape=jax.ShapeDtypeStruct((3, ROWS, WALL * LANES), F32),
        in_specs=[anywhere] * 4 + [pl.BlockSpec(memory_space=pltpu.VMEM), pl.BlockSpec(memory_space=pltpu.SMEM)],
        out_specs=anywhere,
        scratch_shapes=[
            pltpu.VMEM((3, NY + len(DETOUR) * ROWS, LANES), F32),
            pltpu.VMEM((4, NY, LANES), F32),
            pltpu.VMEM((3, NY, LANES), F32),
            pltpu.VMEM((3, NY, LANES), F32),
            pltpu.VMEM((3, NY, LANES), F32),
            pltpu.VMEM((2, NY, NY), F32),
            pltpu.VMEM((2 * NY, 3 * NY), BF16),
            pltpu.VMEM((3 * NY, 2 * LANES), BF16),
            pltpu.VMEM((NY, NY), BF16),
            pltpu.VMEM((NY, 2 * LANES), F32),
            pltpu.VMEM((3, NY, LANES), F32),
            pltpu.SemaphoreType.DMA((3,)),
            pltpu.SemaphoreType.DMA((4,)),
            pltpu.SemaphoreType.DMA((len(CHUNKS) * (WALL + len(DETOUR)),)),
            pltpu.SemaphoreType.DMA((4,)),
            pltpu.SemaphoreType.DMA((len(CHUNKS) * WALL,)),
            pltpu.SemaphoreType.DMA((len(CHUNKS),)),
        ],
        compiler_params=pltpu.CompilerParams(
            collective_id=0, has_side_effects=True, vmem_limit_bytes=40 * 1024 * 1024
        ),
        name="shooting",
    )(start, end_state[0], coupling[0], inverse_ops, mirror_rows.reshape(1, NY), slab_steps)
    return (arrived + start)[None]


def solution(mesh):
    in_specs = (
        P("tm", None, "wall", None),
        P("tm", None, None, "wall"),
        P("tm", None, None, "wall"),
        P("wall", None, None),
        P(),
        P("tm"),
    )
    out_specs = P("tm", None, "wall", None)
    return jax.shard_map(
        on_device, mesh=mesh, in_specs=in_specs, out_specs=out_specs, check_vma=False
    )
```

time: 179 us -> 92.3 us (0.52); the launches traced: 175 us -> 92 us
  Pallas kernels: 0 us -> 85.3 us
  blocking collectives: 40.7 us -> 0 us
  waiting for transfers between devices: 38.7 us -> 0 us
  local copies, waits for them, and re-layouts: 40.1 us -> 5.15 us
  starting transfers between devices: 30 us -> 0 us
  matrix products: 14.4 us -> 0 us
  other arithmetic: 10.4 us -> 0.9 us
    pallas_call x0 -> x1, Pallas kernels: none -> 85.3 us  [on_device(): pl.pallas_call(kernel, out_shape=jax.ShapeDtypeStruct((3, ROWS, WALL * LA...]
    all_to_all x1 -> x0, blocking collectives: 40.7 us -> none  [on_device(): lax.all_to_all(gradient_modes, 'wall', split_axis=2, concat_axis=3, tiled...]
    all_to_all x1 -> x0, waiting for transfers between devices: 26.4 us -> none  [on_device(): lax.all_to_all(following, 'wall', split_axis=3, concat_axis=2, tiled=True)]
    ppermute x2 -> x0, starting transfers between devices: 18.1 us -> none  [shifted(): return lax.ppermute(value, axis, pairs)]
    dot_general x8 -> x0, matrix products: 14.4 us -> none  [helmholtz(): jnp.einsum('gyz,sczgm->scygm', inverse_ops, blocked, precision=lax.Precis...]
    ppermute x2 -> x0, waiting for transfers between devices: 12.3 us -> none  [shifted(): return lax.ppermute(value, axis, pairs)]
    all_to_all x1 -> x0, starting transfers between devices: 11.9 us -> none  [on_device(): lax.all_to_all(following, 'wall', split_axis=3, concat_axis=2, tiled=True)]
    mul x8 -> x0, local copies, waits for them, and re-layouts: 7.94 us -> none  [adjoint(): advanced = helmholtz(coupling * adjoint_state, inverse_ops)]
  transfers between devices with their start and end apart: 3 -> 0, of which waited for: 2 -> 0; matrix products, arithmetic and copies ran while one was open for 18% -> 0% of each run, Pallas kernels for 0% -> 0%
where the time goes in v1:
time: 92.3 us; the launch traced here: 92 us
  Pallas kernels  85.3 us (92%)
  local copies, waits for them, and re-layouts  5.15 us (6%)
    pallas_call x1, Pallas kernels, on_device(): pl.pallas_call(kernel, out_shape=jax.ShapeDtypeStruct((3, ROWS, WALL * LA...  85.3 us
    unnamed x8, local copies, waits for them, and re-layouts  4.46 us

profile of v1, /device:TPU:1, one launch (start us, length us, event | category | flops | bytes accessed | tf_op | source)
XLA Modules:
  0.0 92.0 jit_solution(241991309548892235)
XLA Ops:
  0.7 0.7 reshape.3.mirror_ref
  1.3 0.0 copy-start
  1.3 1.1 %copy-done = f32[1,3,24,2048]{3,2,1,0:T(8,128)S(1)} copy-done((f32[1,3,24,2048]{3,2,1,0:T(8,128)S(1)}, f32[1,3,24,2048]{3,2,1,0:T(8,128)}, u32[]{:S(2)}) %copy-start) | copy-done | bytes 589848
  2.4 0.0 copy-start.1
  2.4 1.3 %copy-done.1 = f32[2,384,384]{2,1,0:T(8,128)S(1)} copy-done((f32[2,384,384]{2,1,0:T(8,128)S(1)}, f32[2,384,384]{2,1,0:T(8,128)}, u32[]{:S(2)}) %copy-start.1) | copy-done | bytes 1179672
  3.7 0.0 copy-start.2
  3.7 1.1 %copy-done.2 = f32[1,3,384,128]{3,2,1,0:T(8,128)S(1)} copy-done((f32[1,3,384,128]{3,2,1,0:T(8,128)S(1)}, f32[1,3,384,128]{3,2,1,0:T(8,128)}, u32[]{:S(2)}) %copy-start.2) | copy-done | bytes 589848
  4.7 0.0 copy-start.3
  4.7 1.1 %copy-done.3 = f32[1,3,384,128]{3,2,1,0:T(8,128)S(1)} copy-done((f32[1,3,384,128]{3,2,1,0:T(8,128)S(1)}, f32[1,3,384,128]{3,2,1,0:T(8,128)}, u32[]{:S(2)}) %copy-start.3) | copy-done | bytes 589848
  5.8 85.3 %shooting.1 = f32[3,24,2048]{2,1,0:T(8,128)S(1)} custom-call(f32[3,24,2048]{2,1,0:T(8,128)S(1)} %bitcast.6, f32[3,384,128]{2,1,0:T(8,128)S(1)} %bitcast.7, f32[3,384,128]{2,1,0:T(8,128)S(1)} %bitcast.8, f32[2,384,384]{2,1,0:T(8,128)S(1)} %copy-done.1, s32[1,384]{1,0:T(1,128)S(1)} %reshape.3.mirror_ref, s32[1]{0:T(128)S(6)} %copy.7.steps_ref), custom_call_target="tpu_custom_call" | custom-call | tf_op jit(solution)/shard_map/shooting/pallas_call | solution.py:268
  91.1 0.9 add_bitcast_fusion
Async XLA Ops:
  1.3 1.1 %copy-start = (f32[1,3,24,2048]{3,2,1,0:T(8,128)S(1)}, f32[1,3,24,2048]{3,2,1,0:T(8,128)}, u32[]{:S(2)}) copy-start(f32[1,3,24,2048]{3,2,1,0:T(8,128)} %param.6) | copy-start | bytes 1769476
  2.4 1.3 %copy-start.1 = (f32[2,384,384]{2,1,0:T(8,128)S(1)}, f32[2,384,384]{2,1,0:T(8,128)}, u32[]{:S(2)}) copy-start(f32[2,384,384]{2,1,0:T(8,128)} %ops_ref.1) | copy-start | bytes 3538948
  3.7 1.1 %copy-start.2 = (f32[1,3,384,128]{3,2,1,0:T(8,128)S(1)}, f32[1,3,384,128]{3,2,1,0:T(8,128)}, u32[]{:S(2)}) copy-start(f32[1,3,384,128]{3,2,1,0:T(8,128)} %param.7) | copy-start | bytes 1769476
  4.7 1.1 %copy-start.3 = (f32[1,3,384,128]{3,2,1,0:T(8,128)S(1)}, f32[1,3,384,128]{3,2,1,0:T(8,128)}, u32[]{:S(2)}) copy-start(f32[1,3,384,128]{3,2,1,0:T(8,128)} %param.8) | copy-start | bytes 1769476

commit v2 on v0

v2 whole, which is shorter than its diff:
```python
import functools

import jax
import jax.numpy as jnp
from jax import lax
from jax.experimental import pallas as pl
from jax.experimental.pallas import tpu as pltpu
from jax.sharding import PartitionSpec as P

STEPS = 8
NY = 384
ROWS = 24
LANES = 128
WALL = 16
CHUNKS = ((0, 2), (2, 1))
OUTGOING = ((0, 1), (1, 2))
SLOTS = ((0, 1), (2, 1))
SIGN = (1.0, -1.0, 1.0)
DETOUR = ((0, 0), (0, 1), (1, 0))
MESH = pl.DeviceIdType.MESH
F32 = jnp.float32
BF16 = jnp.bfloat16


def place():
    tm = lax.axis_index("tm")
    wall = lax.axis_index("wall")
    x = lax.rem(tm, 4)
    y = lax.rem(lax.div(wall, 2), 4)
    core = lax.rem(wall, 2)
    z = lax.div(wall, 8) * 8 + lax.div(tm, 4)
    return x, y, z, core


def halves(value):
    high = value.astype(BF16)
    return high, (value - high.astype(F32)).astype(BF16)


def permuted(onehot, value):
    high = value.astype(BF16)
    rest = value - high.astype(F32)
    middle, low = halves(rest)
    dot = functools.partial(jnp.dot, preferred_element_type=F32)
    return (dot(onehot, high) + dot(onehot, middle)) + dot(onehot, low)


def lane_tile(rows):
    return lax.broadcasted_iota(jnp.int32, (rows, LANES), 1) < 64


def packed(zero, one, lower):
    return (jnp.where(lower, zero, pltpu.roll(one, 64, 1)),
            jnp.where(lower, pltpu.roll(zero, 64, 1), one))


def kernel(start_ref, end_ref, coupling_ref, ops_ref, mirror_ref, steps_ref, out_ref,
           rows_v, pack, land, end_land, end_send, end_v, coup_v, ops_v, mirror_v, wcat, xcat, onehot, state, shared,
           result, local_sem, send_sem, land_sem, end_sem, out_sem, own_sem):
    loads = [
        pltpu.make_async_copy(start_ref, rows_v, local_sem.at[0]),
        pltpu.make_async_copy(mirror_ref, mirror_v, local_sem.at[1]),
        pltpu.make_async_copy(end_ref, end_v, local_sem.at[2]),
        pltpu.make_async_copy(ops_ref, ops_v, local_sem.at[3]),
        pltpu.make_async_copy(coupling_ref, coup_v, local_sem.at[4]),
    ]
    for load in loads:
        load.start()

    x, y, z, core = place()
    tm, wall = lax.axis_index("tm"), lax.axis_index("wall")
    first = x == 0
    last = x == 3
    tm_before, tm_after = lax.rem(tm + 31, 32), lax.rem(tm + 1, 32)

    def upper(height):
        return lax.div(lax.rem(height, 16), 8) * 8

    def column(x_at, height):
        return lax.rem(height, 8) * 4 + x_at

    y_parts = [lax.rem(y + dy, 4) * 2 for dy in range(4)]
    core_parts = [core, 1 - core]
    here = y_parts[0] + core
    behind = jnp.where(first, 1, 0)
    ahead = jnp.where(last, 1, 0)
    halves_to = {half: upper(z + half + 16 - behind) for half in (8, 0)}
    halves_from = {half: upper(z + half + ahead) for half in (8, 0)}
    halves_in = {half: upper(z + half) for half in (8, 0)}
    next_run = lax.rem(lax.div(tm, 4) + 1, 8) * 4
    run_before = lax.rem(lax.div(tm, 4) + 7, 8) * 4

    barrier = pltpu.get_barrier_semaphore()

    def greet(*device):
        pl.semaphore_signal(barrier, inc=1, device_id=device, device_id_type=MESH)

    for other in range(WALL):
        greet(tm_after, other)
    greet(tm_before, wall)

    @pl.when(first)
    def _():
        for dy, dc in DETOUR:
            greet(column(0, z + 2), upper(z + 2) + y_parts[-dy] + core_parts[dc])
        greet(run_before + 1, wall)
        greet(run_before + 2, wall)

    @pl.when(last)
    def _():
        greet(column(0, z + 7), upper(z + 7) + here)

    @pl.when(x == 1)
    def _():
        greet(tm + 2, wall)

    loads[0].wait()
    narrow = lane_tile(ROWS)

    def pack_columns(number, carry):
        lanes = pl.ds(pl.multiple_of(number * LANES, LANES), LANES)
        pack[0, :, lanes], pack[2, :, lanes] = packed(rows_v[0, :, lanes], rows_v[1, :, lanes], narrow)
        pack[1, :, lanes] = rows_v[2, :, lanes]
        return carry

    lax.fori_loop(0, WALL, pack_columns, 0, unroll=4)
    pl.semaphore_wait(barrier, jnp.where(first, WALL + 5, WALL + 2))

    def first_hop(index, half, dy, dc):
        wall_to = halves_to[half] + y_parts[dy] + core_parts[dc]
        lanes = pl.multiple_of(wall_to * LANES, LANES)
        tm_to, row, sem = tm_before, wall * ROWS, index * WALL + wall
        comp, count = CHUNKS[index]
        if half and (dy, dc) in DETOUR:
            comp, count = 0, 3
            number = DETOUR.index((dy, dc))
            tm_to = jnp.where(first, column(0, z + 14), tm_to)
            wall_to = jnp.where(first, upper(z + 14) + y_parts[dy] + core_parts[dc], wall_to)
            row = jnp.where(first, NY + number * ROWS, row)
            sem = jnp.where(first, len(CHUNKS) * WALL + number, sem)
        return pltpu.make_async_remote_copy(
            pack.at[pl.ds(comp, count), :, pl.ds(lanes, LANES)],
            land.at[pl.ds(comp, count), pl.ds(pl.multiple_of(row, 8), ROWS), :],
            send_sem.at[index], land_sem.at[sem], device_id=(tm_to, wall_to), device_id_type=MESH)

    pairs = [(dy, dc) for dy in range(4) for dc in range(2)]
    plain = [(half, dy, dc) for half in (8, 0) for dy, dc in pairs if not half or (dy, dc) not in DETOUR]
    sends = [[first_hop(0, 8, dy, dc) for dy, dc in DETOUR] + [first_hop(0, *offset) for offset in plain]]
    sends += [[first_hop(index, *offset) for offset in plain] for index in range(1, len(CHUNKS))]
    for send in sends[0]:
        send.start()

    lower = lane_tile(NY)
    signs = [jnp.where(lower, SIGN[0], SIGN[1]), SIGN[2], jnp.where(lower, SIGN[0], SIGN[1])]
    source = lax.broadcasted_iota(jnp.int32, (NY, NY), 0)
    loads[1].wait()
    onehot[...] = jnp.where(source == mirror_v[...].reshape(1, NY), 1.0, 0.0).astype(BF16)
    loads[2].wait()
    kept = end_v[2]
    end_v[0], end_v[2] = packed(end_v[0], end_v[1], lower)
    end_v[1] = kept
    end_sends = []
    for comp in (1, 2, 0):
        end_send[comp] = permuted(onehot[...], end_v[comp]) * signs[comp]
        slot, tm_to = comp, tm_after
        if comp:
            tm_to = jnp.where(last, tm - (3 - comp), tm_to)
            slot = jnp.where(last, 3, comp)
        send = pltpu.make_async_remote_copy(
            end_send.at[comp], end_land.at[slot], send_sem.at[len(CHUNKS)], end_sem.at[slot],
            device_id=(tm_to, wall), device_id_type=MESH)
        send.start()
        end_sends.append(send)

    def arrival(ref, sem):
        return pltpu.make_async_remote_copy(
            ref, ref, send_sem.at[len(CHUNKS) + 1], sem, device_id=(tm, wall), device_id_type=MESH)

    def passing(number):
        dy, dc = DETOUR[number]
        wall_from = upper(z + 2) + y_parts[-dy] + core_parts[dc]
        held = land.at[:, pl.ds(NY + number * ROWS, ROWS), :]
        return held, pltpu.make_async_remote_copy(
            held, land.at[:, pl.ds(pl.multiple_of(wall_from * ROWS, 8), ROWS), :],
            send_sem.at[len(CHUNKS) + 1], land_sem.at[wall_from],
            device_id=(column(3, z + 9), upper(z + 9) + here), device_id_type=MESH)

    @pl.when(first)
    def _():
        for number in range(len(DETOUR)):
            held, copy = passing(number)
            arrival(held, land_sem.at[len(CHUNKS) * WALL + number]).wait_recv()
            copy.start()

    loads[3].wait()
    for group in range(2):
        high, low = halves(ops_v[group])
        wcat[group, :, 0:NY] = high
        wcat[group, :, NY:2 * NY] = low
        wcat[group, :, 2 * NY:3 * NY] = high
    loads[4].wait()
    kept = coup_v[2]
    coup_v[0], coup_v[2] = packed(coup_v[0], coup_v[1], lower)
    coup_v[1] = kept

    @pl.when((x == 1) | (x == 2))
    def _():
        arrival(end_land.at[3], end_sem.at[3]).wait_recv()
        pltpu.make_async_remote_copy(
            end_land.at[3], end_land.at[x], send_sem.at[len(CHUNKS) + 1], end_sem.at[x],
            device_id=(next_run, wall), device_id_type=MESH).start()

    for send in sends[0]:
        send.wait_send()
    for send in sends[1]:
        send.start()

    def leaving(index, half, dy, dc):
        comp, count = OUTGOING[index]
        wall_to = halves_in[half] + y_parts[dy] + core_parts[dc]
        return pltpu.make_async_remote_copy(
            result.at[pl.ds(comp, count), pl.ds(pl.multiple_of(wall_to * ROWS, 8), ROWS), :],
            out_ref.at[pl.ds(comp, count), :, pl.ds(pl.multiple_of(wall * LANES, LANES), LANES)],
            send_sem.at[len(CHUNKS) + 2], out_sem.at[index * WALL + wall], device_id=(tm, wall_to), device_id_type=MESH)

    def staying(index):
        comp, count = OUTGOING[index]
        return pltpu.make_async_copy(
            result.at[pl.ds(comp, count), pl.ds(pl.multiple_of(wall * ROWS, 8), ROWS), :],
            out_ref.at[pl.ds(comp, count), :, pl.ds(pl.multiple_of(wall * LANES, LANES), LANES)],
            own_sem.at[index])

    steps = steps_ref[0]
    others = [(half, dy, dc) for half in (8, 0) for dy, dc in pairs if half or dy or dc]
    for index, (comp, count) in enumerate(CHUNKS):
        def landed(half, dy, dc, comp, count):
            wall_from = halves_from[half] + y_parts[-dy] + core_parts[dc]
            arrival(land.at[pl.ds(comp, count), pl.ds(pl.multiple_of(wall_from * ROWS, 8), ROWS), :],
                    land_sem.at[index * WALL + wall_from]).wait_recv()

        if index == 0:
            for dy, dc in DETOUR:
                landed(8, dy, dc, 0, 3)
        for offset in plain:
            landed(*offset, comp, count)
        if 1 < index + 2 < len(CHUNKS):
            for send in sends[index + 2]:
                send.start()
        fresh = SLOTS[index] if not index else SLOTS[index][:1]
        for at, slot in enumerate(SLOTS[index]):
            lanes = slice(at * LANES, (at + 1) * LANES)
            if slot in fresh:
                state[:, lanes] = end_v[slot] - permuted(onehot[...], land[slot, 0:NY, :]) * signs[slot]
                if slot == 1:
                    shared[0] = state[:, lanes]
            else:
                state[:, lanes] = shared[0]

        def step(number, carry, index=index):
            for at, slot in enumerate(SLOTS[index]):
                lanes = slice(at * LANES, (at + 1) * LANES)
                high, low = halves(coup_v[slot] * state[:, lanes])
                xcat[0:NY, lanes] = high
                xcat[NY:2 * NY, lanes] = high
                xcat[2 * NY:3 * NY, lanes] = low
            advanced = jnp.dot(wcat[index], xcat[...], preferred_element_type=F32)
            state[...] = jnp.where(number < steps, advanced, state[...])
            return carry

        lax.fori_loop(0, STEPS, step, 0)
        leave, many = OUTGOING[index]
        for slot in range(leave, leave + many):
            arrival(end_land.at[slot], end_sem.at[slot]).wait_recv()
            if slot == 1:
                value = jnp.where(lower, shared[1], state[:, LANES:])
            else:
                value = state[:, 0:LANES]
            result[slot] = value - end_land[slot]
        if not index:
            shared[1] = state[:, LANES:]
        for offset in others:
            leaving(index, *offset).start()
        staying(index).start()

    for index, (comp, count) in enumerate(OUTGOING):
        staying(index).wait()
        for half, dy, dc in others:
            wall_from = halves_in[half] + y_parts[dy] + core_parts[dc]
            arrival(out_ref.at[pl.ds(comp, count), :, pl.ds(pl.multiple_of(wall_from * LANES, LANES), LANES)],
                    out_sem.at[index * WALL + wall_from]).wait_recv()
            leaving(index, half, dy, dc).wait_send()
    for send in sum(sends[1:], end_sends):
        send.wait_send()

    @pl.when(first)
    def _():
        for number in range(len(DETOUR)):
            passing(number)[1].wait_send()

    @pl.when((x == 1) | (x == 2))
    def _():
        arrival(end_land.at[3], end_sem.at[3]).wait_send()


def finish(arrived_ref, start_ref, out_ref):
    lower = lane_tile(ROWS)
    for at in range(0, arrived_ref.shape[2], LANES):
        lanes = slice(at, at + LANES)
        zero, one = packed(arrived_ref[0, :, lanes], arrived_ref[2, :, lanes], lower)
        out_ref[0, :, lanes] = zero + start_ref[0, :, lanes]
        out_ref[1, :, lanes] = one + start_ref[1, :, lanes]
        out_ref[2, :, lanes] = arrived_ref[1, :, lanes] + start_ref[2, :, lanes]


def on_device(start_state, end_state, coupling, inverse_ops, mirror_rows, slab_steps):
    anywhere = pl.BlockSpec(memory_space=pl.ANY)
    start = start_state[0]
    arrived = pl.pallas_call(
        kernel,
        out_shape=jax.ShapeDtypeStruct((3, ROWS, WALL * LANES), F32),
        in_specs=[anywhere] * 5 + [pl.BlockSpec(memory_space=pltpu.SMEM)],
        out_specs=anywhere,
        scratch_shapes=[
            pltpu.VMEM((3, ROWS, WALL * LANES), F32),
            pltpu.VMEM((3, ROWS, WALL * LANES), F32),
            pltpu.VMEM((3, NY + len(DETOUR) * ROWS, LANES), F32),
            pltpu.VMEM((4, NY, LANES), F32),
            pltpu.VMEM((3, NY, LANES), F32),
            pltpu.VMEM((3, NY, LANES), F32),
            pltpu.VMEM((3, NY, LANES), F32),
            pltpu.VMEM((2, NY, NY), F32),
            pltpu.VMEM((NY,), jnp.int32),
            pltpu.VMEM((2, NY, 3 * NY), BF16),
            pltpu.VMEM((3 * NY, 2 * LANES), BF16),
            pltpu.VMEM((NY, NY), BF16),
            pltpu.VMEM((NY, 2 * LANES), F32),
            pltpu.VMEM((2, NY, LANES), F32),
            pltpu.VMEM((3, NY, LANES), F32),
            pltpu.SemaphoreType.DMA((5,)),
            pltpu.SemaphoreType.DMA((len(CHUNKS) + 3,)),
            pltpu.SemaphoreType.DMA((len(CHUNKS) * WALL + len(DETOUR),)),
            pltpu.SemaphoreType.DMA((4,)),
            pltpu.SemaphoreType.DMA((len(CHUNKS) * WALL,)),
            pltpu.SemaphoreType.DMA((len(CHUNKS),)),
        ],
        compiler_params=pltpu.CompilerParams(
            collective_id=0, has_side_effects=True, vmem_limit_bytes=60 * 1024 * 1024
        ),
        name="shooting",
    )(start, end_state[0], coupling[0], inverse_ops, mirror_rows, slab_steps)
    block = pl.BlockSpec((3, ROWS, 4 * LANES), lambda at: (0, 0, at))
    gradient = pl.pallas_call(
        finish,
        out_shape=jax.ShapeDtypeStruct((3, ROWS, WALL * LANES), F32),
        grid=(WALL // 4,),
        in_specs=[block, block],
        out_specs=block,
        name="finish",
    )(arrived, start)
    return gradient[None]


def solution(mesh):
    in_specs = (
        P("tm", None, "wall", None),
        P("tm", None, None, "wall"),
        P("tm", None, None, "wall"),
        P("wall", None, None),
        P(),
        P("tm"),
    )
    out_specs = P("tm", None, "wall", None)
    return jax.shard_map(
        on_device, mesh=mesh, in_specs=in_specs, out_specs=out_specs, check_vma=False
    )
```

time: 179 us -> 89.3 us (0.50)
  the two profiles are of different devices: /device:TPU:1 before, /device:TPU:123 now
where the time goes in v2:
time: 89.3 us; the launch traced here: 89.1 us
  Pallas kernels  88.4 us (99%)
    pallas_call x1, Pallas kernels, on_device(): pl.pallas_call(kernel, out_shape=jax.ShapeDtypeStruct((3, ROWS, WALL * LA...  84.9 us
    pallas_call x1, Pallas kernels, on_device(): pl.pallas_call(finish, out_shape=jax.ShapeDtypeStruct((3, ROWS, WALL * LA...  3.52 us

profile of v2, /device:TPU:123, one launch (start us, length us, event | category | flops | bytes accessed | tf_op | source)
XLA Modules:
  0.0 89.1 jit_solution(15301857849520615027)
XLA Ops:
  0.7 84.9 %shooting.1.arrived_ref = f32[3,24,2048]{2,1,0:T(8,128)} custom-call(f32[3,24,2048]{2,1,0:T(8,128)} %bitcast.4, f32[3,384,128]{2,1,0:T(8,128)} %bitcast.6, f32[3,384,128]{2,1,0:T(8,128)} %bitcast.7, f32[2,384,384]{2,1,0:T(8,128)} %ops_ref.1, s32[384]{0:T(512)} %mirror_ref.1, s32[1]{0:T(128)S(6)} %copy.7.steps_ref), custom_call_target="tpu_custom_call" | custom-call | tf_op jit(solution)/shard_map/shooting/pallas_call | solution.py:318
  85.6 3.5 %finish.1 = f32[3,24,2048]{2,1,0:T(8,128)} custom-call(f32[3,24,2048]{2,1,0:T(8,128)} %shooting.1.arrived_ref, f32[3,24,2048]{2,1,0:T(8,128)} %bitcast.5), custom_call_target="tpu_custom_call" | custom-call | tf_op jit(solution)/shard_map/finish/pallas_call | solution.py:352

commit v3 on v2

--- a/solution.py
+++ b/solution.py
@@ -203,6 +203,9 @@
     coup_v[0], coup_v[2] = packed(coup_v[0], coup_v[1], lower)
     coup_v[1] = kept
 
+    for send in sends[1]:
+        send.start()
+
     @pl.when((x == 1) | (x == 2))
     def _():
         arrival(end_land.at[3], end_sem.at[3]).wait_recv()
@@ -210,10 +213,6 @@
             end_land.at[3], end_land.at[x], send_sem.at[len(CHUNKS) + 1], end_sem.at[x],
             device_id=(next_run, wall), device_id_type=MESH).start()
 
-    for send in sends[0]:
-        send.wait_send()
-    for send in sends[1]:
-        send.start()
 
     def leaving(index, half, dy, dc):
         comp, count = OUTGOING[index]
@@ -289,7 +288,7 @@
             arrival(out_ref.at[pl.ds(comp, count), :, pl.ds(pl.multiple_of(wall_from * LANES, LANES), LANES)],
                     out_sem.at[index * WALL + wall_from]).wait_recv()
             leaving(index, half, dy, dc).wait_send()
-    for send in sum(sends[1:], end_sends):
+    for send in sum(sends, end_sends):
         send.wait_send()
 
     @pl.when(first)
@@ -348,11 +347,11 @@
         ),
         name="shooting",
     )(start, end_state[0], coupling[0], inverse_ops, mirror_rows, slab_steps)
-    block = pl.BlockSpec((3, ROWS, 4 * LANES), lambda at: (0, 0, at))
+    block = pl.BlockSpec((3, ROWS, 8 * LANES), lambda at: (0, 0, at))
     gradient = pl.pallas_call(
         finish,
         out_shape=jax.ShapeDtypeStruct((3, ROWS, WALL * LANES), F32),
-        grid=(WALL // 4,),
+        grid=(2,),
         in_specs=[block, block],
         out_specs=block,
         name="finish",

time: 89.3 us -> 84.8 us (0.950)
  the two profiles are of different devices: /device:TPU:123 before, /device:TPU:1 now
where the time goes in v3:
time: 84.8 us; the launch traced here: 84.7 us
  Pallas kernels  84 us (99%)
    pallas_call x1, Pallas kernels, on_device(): pl.pallas_call(kernel, out_shape=jax.ShapeDtypeStruct((3, ROWS, WALL * LA...  81.9 us
    pallas_call x1, Pallas kernels, on_device(): pl.pallas_call(finish, out_shape=jax.ShapeDtypeStruct((3, ROWS, WALL * LA...  2.08 us

profile of v3, /device:TPU:1, one launch (start us, length us, event | category | flops | bytes accessed | tf_op | source)
XLA Modules:
  0.0 84.7 jit_solution(12649908100824139492)
XLA Ops:
  0.7 81.9 %shooting.1.arrived_ref = f32[3,24,2048]{2,1,0:T(8,128)} custom-call(f32[3,24,2048]{2,1,0:T(8,128)} %bitcast.4, f32[3,384,128]{2,1,0:T(8,128)} %bitcast.6, f32[3,384,128]{2,1,0:T(8,128)} %bitcast.7, f32[2,384,384]{2,1,0:T(8,128)} %ops_ref.1, s32[384]{0:T(512)} %mirror_ref.1, s32[1]{0:T(128)S(6)} %copy.7.steps_ref), custom_call_target="tpu_custom_call" | custom-call | tf_op jit(solution)/shard_map/shooting/pallas_call | solution.py:317
  82.6 2.1 %finish.1 = f32[3,24,2048]{2,1,0:T(8,128)} custom-call(f32[3,24,2048]{2,1,0:T(8,128)} %shooting.1.arrived_ref, f32[3,24,2048]{2,1,0:T(8,128)} %bitcast.5), custom_call_target="tpu_custom_call" | custom-call | tf_op jit(solution)/shard_map/finish/pallas_call | solution.py:351

commit v4 on v3

--- a/solution.py
+++ b/solution.py
@@ -56,7 +56,7 @@
 
 def kernel(start_ref, end_ref, coupling_ref, ops_ref, mirror_ref, steps_ref, out_ref,
            rows_v, pack, land, end_land, end_send, end_v, coup_v, ops_v, mirror_v, wcat, xcat, onehot, state, shared,
-           result, local_sem, send_sem, land_sem, end_sem, out_sem, own_sem):
+           result, local_sem, send_sem, land_sem, end_sem, out_sem, own_sem, go_sem):
     loads = [
         pltpu.make_async_copy(start_ref, rows_v, local_sem.at[0]),
         pltpu.make_async_copy(mirror_ref, mirror_v, local_sem.at[1]),
@@ -90,6 +90,11 @@
     next_run = lax.rem(lax.div(tm, 4) + 1, 8) * 4
     run_before = lax.rem(lax.div(tm, 4) + 7, 8) * 4
 
+    turns = x == 1
+    leads = turns & (lax.div(tm_before, 4) < 4)
+    trails = turns & (lax.div(tm_before, 4) >= 4)
+    partner = lax.rem(tm + 16, 32)
+
     barrier = pltpu.get_barrier_semaphore()
 
     def greet(*device):
@@ -98,6 +103,10 @@
     for other in range(WALL):
         greet(tm_after, other)
     greet(tm_before, wall)
+
+    @pl.when(trails)
+    def _():
+        greet(partner, wall)
 
     @pl.when(first)
     def _():
@@ -124,7 +133,7 @@
         return carry
 
     lax.fori_loop(0, WALL, pack_columns, 0, unroll=4)
-    pl.semaphore_wait(barrier, jnp.where(first, WALL + 5, WALL + 2))
+    pl.semaphore_wait(barrier, jnp.where(first, WALL + 5, WALL + 2) + jnp.where(leads, 1, 0))
 
     def first_hop(index, half, dy, dc):
         wall_to = halves_to[half] + y_parts[dy] + core_parts[dc]
@@ -147,8 +156,16 @@
     plain = [(half, dy, dc) for half in (8, 0) for dy, dc in pairs if not half or (dy, dc) not in DETOUR]
     sends = [[first_hop(0, 8, dy, dc) for dy, dc in DETOUR] + [first_hop(0, *offset) for offset in plain]]
     sends += [[first_hop(index, *offset) for offset in plain] for index in range(1, len(CHUNKS))]
+    @pl.when(trails)
+    def _():
+        pl.semaphore_wait(go_sem, 1)
+
     for send in sends[0]:
         send.start()
+
+    @pl.when(leads)
+    def _():
+        pl.semaphore_signal(go_sem, inc=1, device_id=(partner, wall), device_id_type=MESH)
 
     lower = lane_tile(NY)
     signs = [jnp.where(lower, SIGN[0], SIGN[1]), SIGN[2], jnp.where(lower, SIGN[0], SIGN[1])]
@@ -341,6 +358,7 @@
             pltpu.SemaphoreType.DMA((4,)),
             pltpu.SemaphoreType.DMA((len(CHUNKS) * WALL,)),
             pltpu.SemaphoreType.DMA((len(CHUNKS),)),
+            pltpu.SemaphoreType.REGULAR,
         ],
         compiler_params=pltpu.CompilerParams(
             collective_id=0, has_side_effects=True, vmem_limit_bytes=60 * 1024 * 1024

time: 84.8 us -> 84.1 us (level)
  Pallas kernels: 84 us -> 83.1 us
    pallas_call x1, Pallas kernels: 81.9 us -> 81 us  [on_device(): pl.pallas_call(kernel, out_shape=jax.ShapeDtypeStruct((3, ROWS, WALL * LA...]
where the time goes in v4:
time: 84.1 us; the launch traced here: 83.7 us
  Pallas kernels  83.1 us (99%)
    pallas_call x1, Pallas kernels, on_device(): pl.pallas_call(kernel, out_shape=jax.ShapeDtypeStruct((3, ROWS, WALL * LA...  81 us
    pallas_call x1, Pallas kernels, on_device(): pl.pallas_call(finish, out_shape=jax.ShapeDtypeStruct((3, ROWS, WALL * LA...  2.08 us

profile of v4, /device:TPU:1, one launch (start us, length us, event | category | flops | bytes accessed | tf_op | source)
XLA Modules:
  0.0 83.7 jit_solution(13164558043035457971)
XLA Ops:
  0.7 81.0 %shooting.1.arrived_ref = f32[3,24,2048]{2,1,0:T(8,128)} custom-call(f32[3,24,2048]{2,1,0:T(8,128)} %bitcast.4, f32[3,384,128]{2,1,0:T(8,128)} %bitcast.6, f32[3,384,128]{2,1,0:T(8,128)} %bitcast.7, f32[2,384,384]{2,1,0:T(8,128)} %ops_ref.1, s32[384]{0:T(512)} %mirror_ref.1, s32[1]{0:T(128)S(6)} %copy.7.steps_ref), custom_call_target="tpu_custom_call" | custom-call | tf_op jit(solution)/shard_map/shooting/pallas_call | solution.py:334
  81.7 2.1 %finish.1 = f32[3,24,2048]{2,1,0:T(8,128)} custom-call(f32[3,24,2048]{2,1,0:T(8,128)} %shooting.1.arrived_ref, f32[3,24,2048]{2,1,0:T(8,128)} %bitcast.5), custom_call_target="tpu_custom_call" | custom-call | tf_op jit(solution)/shard_map/finish/pallas_call | solution.py:369

commit v5 on v4

--- a/solution.py
+++ b/solution.py
@@ -64,8 +64,7 @@
         pltpu.make_async_copy(ops_ref, ops_v, local_sem.at[3]),
         pltpu.make_async_copy(coupling_ref, coup_v, local_sem.at[4]),
     ]
-    for load in loads:
-        load.start()
+    loads[0].start()
 
     x, y, z, core = place()
     tm, wall = lax.axis_index("tm"), lax.axis_index("wall")
@@ -123,6 +122,8 @@
     def _():
         greet(tm + 2, wall)
 
+    for load in loads[1:]:
+        load.start()
     loads[0].wait()
     narrow = lane_tile(ROWS)
 

time: 84.1 us -> 84.1 us (level)
  no operation moved by 1% of the time
where the time goes in v5:
time: 84.1 us; the launch traced here: 83.7 us
  Pallas kernels  83.1 us (99%)
    pallas_call x1, Pallas kernels, on_device(): pl.pallas_call(kernel, out_shape=jax.ShapeDtypeStruct((3, ROWS, WALL * LA...  81 us
    pallas_call x1, Pallas kernels, on_device(): pl.pallas_call(finish, out_shape=jax.ShapeDtypeStruct((3, ROWS, WALL * LA...  2.08 us

profile of v5, /device:TPU:1, one launch (start us, length us, event | category | flops | bytes accessed | tf_op | source)
XLA Modules:
  0.0 83.7 jit_solution(10071727732046041106)
XLA Ops:
  0.7 81.0 %shooting.1.arrived_ref = f32[3,24,2048]{2,1,0:T(8,128)} custom-call(f32[3,24,2048]{2,1,0:T(8,128)} %bitcast.4, f32[3,384,128]{2,1,0:T(8,128)} %bitcast.6, f32[3,384,128]{2,1,0:T(8,128)} %bitcast.7, f32[2,384,384]{2,1,0:T(8,128)} %ops_ref.1, s32[384]{0:T(512)} %mirror_ref.1, s32[1]{0:T(128)S(6)} %copy.7.steps_ref), custom_call_target="tpu_custom_call" | custom-call | tf_op jit(solution)/shard_map/shooting/pallas_call | solution.py:335
  81.7 2.1 %finish.1 = f32[3,24,2048]{2,1,0:T(8,128)} custom-call(f32[3,24,2048]{2,1,0:T(8,128)} %shooting.1.arrived_ref, f32[3,24,2048]{2,1,0:T(8,128)} %bitcast.5), custom_call_target="tpu_custom_call" | custom-call | tf_op jit(solution)/shard_map/finish/pallas_call | solution.py:370
